TPU v7x, 128 devices: a whole 4x4x4 slice. The times are simulated.
128 devices in a mesh: tile: 16 (over x, y), view: 8 (over z, core).
Axes of the slice: x: 4, y: 4, z: 4, core: 2. Of those that a mesh axis runs over, the one named last changes fastest.
Arguments:
- estimate: float32 [2, 224, 448, 128], P(None, 'view', 'tile'), may hold values from 0.25 to 4
- view_data: bfloat16 [8, 16, 3, 2, 58, 58, 128], P('view', 'tile'), may hold values from 0.25 to 4
- psf: float32 [6, 3, 31], replicated, may hold values from 0 to 0.5, as said below
- background: float32 [6], replicated, may hold values from 0.1 to 1
- slot_brick: int32 [8, 16, 3], P('view', 'tile'), may hold values from 0 to 15, as said below
- slot_view: int32 [8, 16, 3], P('view', 'tile'), may hold values from 0 to 5, as said below
- intersection: int32 [8, 16, 6], P('view', 'tile'), may hold values from 0 to 1, as said below
Outputs:
- updated: float32 [2, 224, 448, 128], P(None, 'view', 'tile')
Inputs may be any that keep to these rules, and one draw needn't show every extreme that they name: `slot_brick`: within a group, the jobs are exactly the pairs (brick, view) that intersection marks, each once; every brick has at least one view and one brick of each group has all 6; the jobs of a group fill its workers' 3 slots exactly. `slot_view`: the view of each job, consistent with intersection. `intersection`: each brick's row has between 1 and 6 ones. `psf`: all taps are positive.
All inputs are finite; a program needn't handle non-finite values.
Results may differ from a plain program's by a relative error of at most 0.0003.
Values may be sent and summed in bfloat16 or wider, within the bound.
No kernel may reach another device: no remote copies, remote signals or barrier semaphores. Data moves between devices by JAX's collectives and lax.ppermute only.
A program may use at most 128 MiB of HBM per device.

v0:
```python
import jax
import jax.numpy as jnp
from jax import lax
from jax.sharding import PartitionSpec as P


def extended(array, sides, width):
    for axis, dim in sides:
        count, length = (lax.axis_size(axis), array.shape[dim])
        up = [(i, (i + 1) % count) for i in range(count - 1)]
        down = [(j, i) for i, j in up]
        last = lax.slice_in_dim(array, length - width, length, axis=dim)
        leading = lax.slice_in_dim(array, 0, width, axis=dim)
        before = lax.ppermute(last, axis, up)
        after = lax.ppermute(leading, axis, down)
        array = jnp.concatenate([before, array, after], axis=dim)
    return array


def banded(kernel_taps, order, rim_width):
    offsets = jnp.arange(order)[None, :] - jnp.arange(order)[:, None] + rim_width
    matches = offsets[:, :, None] == jnp.arange(kernel_taps.shape[0])[None, None, :]
    return jnp.sum(jnp.where(matches, kernel_taps[None, None, :], 0.0), axis=2)


def forward_blur(block, kernels, rim_width):
    band_x = banded(kernels[0], block.shape[1], rim_width)
    band_y = banded(kernels[1], block.shape[2], rim_width)
    band_z = banded(kernels[2], block.shape[3], rim_width)
    result = jnp.einsum("cxyz,wz->cxyw", block, band_z, precision=lax.Precision.HIGHEST)
    result = jnp.einsum("cxyz,vy->cxvz", result, band_y, precision=lax.Precision.HIGHEST)
    return jnp.einsum("cxyz,ux->cuyz", result, band_x, precision=lax.Precision.HIGHEST)


def backward_blur(ratio, kernels, rim_width, brick_x, brick_y):
    band_x = banded(kernels[0], ratio.shape[1], rim_width)[:, rim_width : rim_width + brick_x]
    band_y = banded(kernels[1], ratio.shape[2], rim_width)[:, rim_width : rim_width + brick_y]
    band_z = banded(kernels[2], ratio.shape[3], rim_width)
    result = jnp.einsum("cxyz,xu->cuyz", ratio, band_x, precision=lax.Precision.HIGHEST)
    result = jnp.einsum("cxyz,yv->cxvz", result, band_y, precision=lax.Precision.HIGHEST)
    return jnp.einsum("cxyz,zw->cxyw", result, band_z, precision=lax.Precision.HIGHEST)


def correction(block, measured, psf, background, view_index, rim_width, brick_x, brick_y):
    kernels = lax.dynamic_index_in_dim(psf, view_index, 0, keepdims=False)
    backdrop = lax.dynamic_index_in_dim(background, view_index, 0, keepdims=False)
    predicted = forward_blur(block, kernels, rim_width) + backdrop
    ratio = measured.astype(jnp.float32) / predicted
    return backward_blur(ratio, kernels, rim_width, brick_x, brick_y)


def on_device(estimate, view_data, psf, background, slot_brick, slot_view, intersection):
    rim_width = psf.shape[2] // 2
    channels, brick_x, brick_y, depth_cells = estimate.shape
    est_wire = estimate.astype(jnp.bfloat16)
    padded = extended(est_wire, (("tile", 2), ("view", 1)), rim_width)
    gathered = lax.all_gather(padded[None], "tile", axis=0, tiled=True)
    owners = lax.axis_size("tile")
    contrib = jnp.zeros((owners, channels, brick_x, brick_y, depth_cells), jnp.float32)
    for slot_index in range(slot_brick.shape[2]):
        brick_index = slot_brick[0, 0, slot_index]
        view_index = slot_view[0, 0, slot_index]
        block = lax.dynamic_index_in_dim(gathered, brick_index, 0, keepdims=False).astype(
            jnp.float32
        )
        factor = correction(
            block,
            view_data[0, 0, slot_index],
            psf,
            background,
            view_index,
            rim_width,
            brick_x,
            brick_y,
        )
        owner_marks = (jnp.arange(owners) == brick_index).astype(jnp.float32)
        contrib = contrib + owner_marks[:, None, None, None, None] * factor[None]
    summed = lax.psum_scatter(contrib, "tile", scatter_dimension=0, tiled=True)[0]
    views_seen = jnp.sum(intersection[0, 0]).astype(jnp.float32)
    return estimate * summed / views_seen


def solution(mesh):
    placed = (
        P(None, "view", "tile", None),
        P("view", "tile", None, None, None, None, None),
        P(),
        P(),
        P("view", "tile", None),
        P("view", "tile", None),
        P("view", "tile", None),
    )
    return jax.shard_map(
        on_device,
        mesh=mesh,
        in_specs=placed,
        out_specs=P(None, "view", "tile", None),
        check_vma=False,
    )
```

profile of v0, /device:TPU:1, one launch (start us, length us, event | category | flops | bytes accessed | tf_op | source)
XLA Modules:
  0.0 482.3 jit_solution(7533203977830049392)
XLA Ops:
  6.5 0.0 all-gather.3.cloned.1.call-start
  6.5 1.2 copy.95
  7.8 0.1 fusion.61
  7.9 4.0 collective-permute-start
  11.9 1.3 collective-permute-start.1
  13.2 2.9 collective-permute-done
  16.2 3.8 collective-permute-done.1
  20.0 0.3 pad_maximum_fusion.1
  20.3 0.0 copy-start.9
  20.3 0.0 copy-start.10
  20.3 0.0 copy-start.11
  20.4 0.0 copy-start.12
  20.4 0.1 fusion.60
  20.5 5.3 %collective-permute-start.2 = (bf16[2,15,58,128]{3,2,1,0:T(8,128)(2,1)S(1)}, bf16[2,15,58,128]{3,2,1,0:T(8,128)(2,1)S(1)}, u32[]{:S(2)}, u32[]{:S(2)}) collective-permute-start(bf16[2,15,58,128]{3,2,1,0:T(8,128)(2,1)S(1)} %get-tuple-element.17), channel_id=1, source_target_pairs={{0,1},{1,2},{2,3},{3,4},{4,5},{5,6},{6,7},{8,9},{9,10},{10,11},{11... | collective-permute-start | bytes 1336328 | tf_op jit(solution)/shard_map/ppermute | solution.py:14
  25.8 1.9 collective-permute-start.3
  27.7 3.8 collective-permute-done.2
  31.5 4.4 collective-permute-done.3
  35.9 1.8 pad_maximum_fusion
  37.7 0.0 all-gather.3.cloned.1.call-update
  37.7 0.0 all-reduce.3.cloned.1.call-start
  37.8 0.0 copy-done.9
  37.8 0.6 fusion.63
  42.0 0.0 copy-done.10
  42.0 0.6 fusion.64
  49.9 0.7 fusion.62
  50.5 1.2 compare_convert_fusion.2
  51.8 1.2 compare_convert_fusion
  53.1 2.0 select_reduce_fusion.7
  55.0 1.2 select_reduce_fusion.2
  56.3 6.5 %fusion.59 = (bf16[1,1,1,2,58,58,128]{6,3,5,4,2,1,0:T(2,128)(2,1)S(1)}, bf16[1,1,1,2,58,58,128]{6,3,5,4,2,1,0:T(2,128)(2,1)S(1)}, bf16[1,1,1,2,58,58,128]{6,3,5,4,2,1,0:T(2,128)(2,1)}) fusion(bf16[1,1,3,2,58,58,128]{6,3,5,4,2,1,0:T(2,128)(2,1)} %param.8), kind=kLoop, calls=%fused_computation.101 | loop fusion | bytes 10334208 | tf_op jit(solution)/shard_map/slice | solution.py:68
  62.8 158.6 %all-gather.3.cloned.1.call-done = bf16[32,58,58,128]{3,2,1,0:T(8,128)(2,1)} async-done(((bf16[2,58,58,128]{3,2,1,0:T(8,128)(2,1)}), bf16[32,58,58,128]{3,2,1,0:T(8,128)(2,1)}) %all-gather.3.cloned.1.call-update) | async-done | bytes 27557904 | tf_op jit(solution)/shard_map/all_gather | solution.py:57
  221.3 3.2 fusion.9
  224.6 3.7 convolution_bitcast_fusion
  228.3 5.5 %fusion = f32[58,2,58,128]{3,0,2,1:T(8,128)S(1)} fusion(f32[2,58,58,128]{3,2,1,0:T(8,128)S(1)} %convolution_bitcast_fusion, f32[58,58]{1,0:T(8,128)S(1)} %copy-done.8), kind=kOutput, calls=%fused_computation.4 | convolution fusion | flops 599384064 | bytes 6902928 | tf_op jit(solution)/shard_map/cxyz,ux->cuyz/dot_general | solution.py:32
  233.7 0.0 copy-start.3
  233.8 3.6 fusion.27
  237.4 2.0 fusion.36
  239.4 0.0 copy-done.3
  239.4 0.9 fusion.41
  240.3 0.6 copy.33
  240.9 3.2 fusion.13
  244.2 3.7 convolution_bitcast_fusion.2
  247.9 0.0 copy-done.7
  247.9 5.9 %fusion.4 = f32[58,2,58,128]{3,0,2,1:T(8,128)S(1)} fusion(f32[2,58,58,128]{3,2,1,0:T(8,128)S(1)} %convolution_bitcast_fusion.2, f32[58,58]{1,0:T(8,128)S(1)} %copy-done.7), kind=kOutput, calls=%fused_computation.8 | convolution fusion | flops 599384064 | bytes 6902928 | tf_op jit(solution)/shard_map/cxyz,ux->cuyz/dot_general | solution.py:32
  253.8 3.4 fusion.29
  257.2 2.0 fusion.30
  259.3 0.0 copy-done.2
  259.3 3.2 fusion.11
  262.5 3.8 convolution_bitcast_fusion.1
  266.4 5.5 %fusion.2 = f32[58,2,58,128]{3,0,2,1:T(8,128)S(1)} fusion(f32[2,58,58,128]{3,2,1,0:T(8,128)S(1)} %convolution_bitcast_fusion.1, f32[58,58]{1,0:T(8,128)S(1)} %copy-done.6), kind=kOutput, calls=%fused_computation.6 | convolution fusion | flops 599384064 | bytes 6902928 | tf_op jit(solution)/shard_map/cxyz,ux->cuyz/dot_general | solution.py:32
  271.9 3.4 fusion.28
  275.3 2.0 fusion.33
  277.3 0.9 fusion.44
  278.2 0.6 copy.27
  278.9 1.1 fusion.47
  280.0 0.6 copy.21
  280.6 10.7 %multiply_add_fusion = f32[16,2,28,28,128]{4,1,3,2,0:T(2,128)} fusion(f32[2,28,28,128]{3,0,2,1:T(2,128)S(1)} %copy.33, f32[2,28,28,128]{3,0,2,1:T(2,128)S(1)} %copy.27, f32[2,28,28,128]{3,0,2,1:T(2,128)S(1)} %copy.21, f32[16]{0:T(128)S(1)} %get-tuple-element.45, f32[16]{0:T(128)S(1)} %get-tuple-element.46, f32[16]{0:T(128)S(1)} %copy-done.13), kind=kLoop, calls=%fused_computation | loop fusion | flops 16056320 | bytes 15253696 | tf_op jit(solution)/shard_map/add | solution.py:77
  291.3 0.0 all-reduce.3.cloned.1.call-update
  291.3 0.6 copy-done.14
  292.0 0.6 reduce_sum.104
  293.3 0.0 copy-done.15
  293.3 0.6 dynamic-slice
  293.9 178.2 %all-reduce.3.cloned.1.call-done = f32[16,2,28,28,128]{4,1,3,2,0:T(2,128)} async-done(((f32[16,2,28,28,128]{4,1,3,2,0:T(2,128)}), f32[16,2,28,28,128]{4,1,3,2,0:T(2,128)}) %all-reduce.3.cloned.1.call-update) | async-done | bytes 12845072
  472.1 3.1 fusion.40
  (25 shorter events, 0.1 us)
Async XLA Ops:
  6.5 214.8 %all-gather.3.cloned.1.call-start = ((), (), s32[]{:S(2)}) async-start(), calls=%async_computation | async-start | bytes 32309248 | tf_op jit(solution)/shard_map/all_gather | solution.py:57
  7.9 8.3 %collective-permute-start = (bf16[2,28,15,128]{3,2,1,0:T(8,128)(2,1)S(1)}, bf16[2,28,15,128]{3,2,1,0:T(8,128)(2,1)S(1)}, u32[]{:S(2)}, u32[]{:S(2)}) collective-permute-start(bf16[2,28,15,128]{3,2,1,0:T(8,128)(2,1)S(1)} %get-tuple-element.19), channel_id=1, source_target_pairs={{0,8},{8,16},{16,24},{24,32},{32,40},{40,48},{48,56},{56,64},{64,7... | collective-permute-start | bytes 645128 | tf_op jit(solution)/shard_map/ppermute | solution.py:14
  11.9 8.0 %collective-permute-start.1 = (bf16[2,28,15,128]{3,2,1,0:T(8,128)(2,1)S(1)}, bf16[2,28,15,128]{3,2,1,0:T(8,128)(2,1)S(1)}, u32[]{:S(2)}, u32[]{:S(2)}) collective-permute-start(bf16[2,28,15,128]{3,2,1,0:T(8,128)(2,1)S(1)} %get-tuple-element.20), channel_id=1, source_target_pairs={{8,0},{16,8},{24,16},{32,24},{40,32},{48,40},{56,48},{64,56},{72,6... | collective-permute-start | bytes 645128 | tf_op jit(solution)/shard_map/ppermute | solution.py:15
  20.3 17.4 %copy-start.9 = (s32[1,1,3]{2,1,0:T(1,128)S(1)}, s32[1,1,3]{2,1,0:T(1,128)}, u32[]{:S(2)}) copy-start(s32[1,1,3]{2,1,0:T(1,128)} %param.11) | copy-start | bytes 40
  20.3 21.7 %copy-start.10 = (s32[1,1,3]{2,1,0:T(1,128)S(1)}, s32[1,1,3]{2,1,0:T(1,128)}, u32[]{:S(2)}) copy-start(s32[1,1,3]{2,1,0:T(1,128)} %param.12) | copy-start | bytes 40
  20.3 29.5 %copy-start.11 = (f32[6]{0:T(128)S(1)}, f32[6]{0:T(128)}, u32[]{:S(2)}) copy-start(f32[6]{0:T(128)} %param.10) | copy-start | bytes 76
  20.4 32.6 %copy-start.12 = (f32[6,3,31]{2,1,0:T(4,128)S(1)}, f32[6,3,31]{2,1,0:T(4,128)}, u32[]{:S(2)}) copy-start(f32[6,3,31]{2,1,0:T(4,128)} %param.9) | copy-start | bytes 6700
  20.5 11.1 %collective-permute-start.2 = (bf16[2,15,58,128]{3,2,1,0:T(8,128)(2,1)S(1)}, bf16[2,15,58,128]{3,2,1,0:T(8,128)(2,1)S(1)}, u32[]{:S(2)}, u32[]{:S(2)}) collective-permute-start(bf16[2,15,58,128]{3,2,1,0:T(8,128)(2,1)S(1)} %get-tuple-element.17), channel_id=1, source_target_pairs={{0,1},{1,2},{2,3},{3,4},{4,5},{5,6},{6,7},{8,9},{9,10},{10,11},{11... | collective-permute-start | bytes 1336328 | tf_op jit(solution)/shard_map/ppermute | solution.py:14
  25.8 10.1 %collective-permute-start.3 = (bf16[2,15,58,128]{3,2,1,0:T(8,128)(2,1)S(1)}, bf16[2,15,58,128]{3,2,1,0:T(8,128)(2,1)S(1)}, u32[]{:S(2)}, u32[]{:S(2)}) collective-permute-start(bf16[2,15,58,128]{3,2,1,0:T(8,128)(2,1)S(1)} %get-tuple-element.18), channel_id=1, source_target_pairs={{1,0},{2,1},{3,2},{4,3},{5,4},{6,5},{7,6},{9,8},{10,9},{11,10},{12... | collective-permute-start | bytes 1336328 | tf_op jit(solution)/shard_map/ppermute | solution.py:15
  37.7 434.4 %all-reduce.3.cloned.1.call-start = ((), (), s32[]{:S(2)}) async-start(), calls=%async_computation.1 | async-start | bytes 25690112
  221.3 3.3 copy-start.5
  224.6 3.7 copy-start.8
  228.3 5.5 %copy-start.1 = (bf16[1,1,1,2,58,58,128]{6,3,5,4,2,1,0:T(2,128)(2,1)S(1)}, bf16[1,1,1,2,58,58,128]{6,3,5,4,2,1,0:T(2,128)(2,1)}, u32[]{:S(2)}) copy-start(bf16[1,1,1,2,58,58,128]{6,3,5,4,2,1,0:T(2,128)(2,1)} %get-tuple-element.16) | copy-start | bytes 5167108
  233.7 5.7 %copy-start.3 = (f32[128,128]{1,0:T(8,128)S(1)}, f32[128,128]{1,0:T(8,128)}, u32[]{:S(2)}) copy-start(f32[128,128]{1,0:T(8,128)} %get-tuple-element.6) | copy-start | bytes 196612
  240.3 3.9 copy-start.4
  244.2 3.7 copy-start.7
  253.8 5.5 %copy-start.2 = (f32[128,128]{1,0:T(8,128)S(1)}, f32[128,128]{1,0:T(8,128)}, u32[]{:S(2)}) copy-start(f32[128,128]{1,0:T(8,128)} %get-tuple-element.7) | copy-start | bytes 196612
  262.5 3.9 copy-start.6
  277.3 3.3 copy-start.13
  291.3 0.7 copy-start.14
  291.3 1.9 copy-start.15
  291.3 180.8 %copy-start = (f32[2,28,28,128]{3,0,2,1:T(2,128)S(1)}, f32[2,28,28,128]{3,0,2,1:T(2,128)}, u32[]{:S(2)}) copy-start(f32[2,28,28,128]{3,0,2,1:T(2,128)} %param.7) | copy-start | bytes 2408452
Sparse Core Ops, SparseCore 0:
  37.8 183.4 all-gather.2
  291.5 180.6 all-reduce.2
where the time goes:
time: 487 us; the launch traced here: 482 us
  waiting for transfers between devices  352 us (72%)
  matrix products  57.1 us (12%)
  between operations  25.6 us (5%)
  other arithmetic  22.1 us (5%)
  local copies, waits for them, and re-layouts  13 us (3%)
  starting transfers between devices  12.6 us (3%)
    unnamed x3, waiting for transfers between devices  178 us
    all_gather x1, waiting for transfers between devices, on_device(): gathered = lax.all_gather(padded[None], 'tile', axis=0, tiled=True)  159 us
    dot_general x3, matrix products, forward_blur(): jnp.einsum('cxyz,ux->cuyz', result, band_x, precision=lax.Precision.HIGHEST)  16.8 us
    dot_general x3, matrix products, forward_blur(): jnp.einsum('cxyz,vy->cxvz', result, band_y, precision=lax.Precision.HIGHEST)  11.1 us
    add x1, other arithmetic, on_device(): contrib = contrib + owner_marks[:, None, None, None, None] * factor[None]  10.7 us
    dot_general x3, matrix products, backward_blur(): jnp.einsum('cxyz,xu->cuyz', ratio, band_x, precision=lax.Precision.HIGHEST)  10.5 us
  transfers between devices with their start and end apart: 6, of which 6 were waited for; matrix products, arithmetic and copies ran while one was open for 3% of the time, Pallas kernels for 0%

commit v1 on v0

--- a/solution.py
+++ b/solution.py
@@ -54,7 +54,16 @@
     channels, brick_x, brick_y, depth_cells = estimate.shape
     est_wire = estimate.astype(jnp.bfloat16)
     padded = extended(est_wire, (("tile", 2), ("view", 1)), rim_width)
-    gathered = lax.all_gather(padded[None], "tile", axis=0, tiled=True)
+    ways = lax.axis_size("tile")
+    up_2 = [(d, (d + 1) % ways) for d in range(ways)]
+    down_2 = [(d, (d - 1) % ways) for d in range(ways)]
+    earlier, later = ([padded[None]], [padded[None]])
+    for _ in range(ways // 2):
+        earlier.append(lax.ppermute(earlier[-1], "tile", up_2))
+    for _ in range((ways - 1) // 2):
+        later.append(lax.ppermute(later[-1], "tile", down_2))
+    line = jnp.concatenate([*earlier[::-1], *later[1:]], axis=0)
+    gathered = jnp.roll(line, (lax.axis_index("tile") - ways // 2) * padded[None].shape[0], axis=0)
     owners = lax.axis_size("tile")
     contrib = jnp.zeros((owners, channels, brick_x, brick_y, depth_cells), jnp.float32)
     for slot_index in range(slot_brick.shape[2]):

time: 487 us -> 804 us (1.65)
  local copies, waits for them, and re-layouts: 13 us -> 112 us
  waiting for transfers between devices: 352 us -> 451 us
  other arithmetic: 22.1 us -> 104 us
  starting transfers between devices: 12.6 us -> 49.6 us
    ppermute x0 -> x15, waiting for transfers between devices: none -> 257 us  [the longest x8 253 us: on_device(): earlier.append(lax.ppermute(earlier[-1], 'tile', up_2))]
    all_gather x1 -> x0, waiting for transfers between devices: 159 us -> none  [on_device(): gathered = lax.all_gather(padded[None], 'tile', axis=0, tiled=True)]
    unnamed x34 -> x76, local copies, waits for them, and re-layouts: 2.52 us -> 90.2 us
    unnamed x0 -> x2, other arithmetic: none -> 58.2 us
    ppermute x0 -> x15, starting transfers between devices: none -> 37.1 us  [the longest x7 35.5 us: on_device(): later.append(lax.ppermute(later[-1], 'tile', down_2))]
    broadcast_in_dim x0 -> x1, other arithmetic: none -> 22.1 us  [on_device(): earlier, later = ([padded[None]], [padded[None]])]
    unnamed x3 -> x2, waiting for transfers between devices: 178 us -> 180 us
  transfers between devices with their start and end apart: 6 -> 20, of which waited for: 6 -> 16; matrix products, arithmetic and copies ran while one was open for 3% -> 12% of each run, Pallas kernels for 0% -> 0%
where the time goes in v1:
time: 804 us; the launch traced here: 795 us
  waiting for transfers between devices  451 us (56%)
  local copies, waits for them, and re-layouts  112 us (14%)
  other arithmetic  104 us (13%)
  matrix products  52.1 us (6%)
  starting transfers between devices  49.6 us (6%)
  between operations  26.4 us (3%)
    ppermute x8, waiting for transfers between devices, on_device(): earlier.append(lax.ppermute(earlier[-1], 'tile', up_2))  253 us
    unnamed x2, waiting for transfers between devices  180 us
    unnamed x76, local copies, waits for them, and re-layouts  90.2 us
    unnamed x2, other arithmetic  58.2 us
    ppermute x7, starting transfers between devices, on_device(): later.append(lax.ppermute(later[-1], 'tile', down_2))  35.5 us
    broadcast_in_dim x1, other arithmetic, on_device(): earlier, later = ([padded[None]], [padded[None]])  22.1 us
    dot_general x3, matrix products, forward_blur(): jnp.einsum('cxyz,ux->cuyz', result, band_x, precision=lax.Precision.HIGHEST)  16.5 us
  transfers between devices with their start and end apart: 20, of which 16 were waited for; matrix products, arithmetic and copies ran while one was open for 12% of the time, Pallas kernels for 0%

profile of v1, /device:TPU:1, one launch (start us, length us, event | category | flops | bytes accessed | tf_op | source)
XLA Modules:
  0.0 794.9 jit_solution(3768481759976465915)
XLA Ops:
  8.3 4.0 collective-permute-start
  13.6 2.6 collective-permute-done
  16.3 3.8 collective-permute-done.1
  21.9 5.3 collective-permute-start.2
  29.1 3.3 collective-permute-done.2
  32.5 4.4 collective-permute-done.3
  36.9 22.1 %maximum_bitcast_fusion = bf16[1,2,58,58,128]{4,1,3,2,0:T(2,128)(2,1)S(1)} fusion(bf16[2,15,58,128]{3,0,2,1:T(2,128)(2,1)S(1)} %collective-permute-done.3, bf16[2,28,15,128]{3,0,2,1:T(2,128)(2,1)S(1)} %collective-permute-done.1, bf16[2,28,28,128]{3,0,2,1:T(2,128)(2,1)S(1)} %convert_element_type.51, bf16[2,28,15,128]{3,0,2,1:T(2,128)(2,1)S(1)} %collective-permute-done, ...), kind=kLoop, calls=%fused_computation.41 | loop fusion | flops 3444736 | bytes 3444736 | tf_op jit(solution)/shard_map/broadcast_in_dim | solution.py:60
  60.3 35.9 %collective-permute-done.4 = bf16[1,2,58,58,128]{4,1,3,2,0:T(2,128)(2,1)S(1)} collective-permute-done((bf16[1,2,58,58,128]{4,1,3,2,0:T(2,128)(2,1)S(1)}, bf16[1,2,58,58,128]{4,1,3,2,0:T(2,128)(2,1)S(1)}, u32[]{:S(2)}, u32[]{:S(2)}) %collective-permute-start.4) | collective-permute-done | bytes 1722400 | tf_op jit(solution)/shard_map/ppermute | solution.py:62
  96.2 4.8 collective-permute-start.12
  101.0 33.4 %collective-permute-done.5 = bf16[1,2,58,58,128]{4,1,3,2,0:T(2,128)(2,1)S(1)} collective-permute-done((bf16[1,2,58,58,128]{4,1,3,2,0:T(2,128)(2,1)S(1)}, bf16[1,2,58,58,128]{4,1,3,2,0:T(2,128)(2,1)S(1)}, u32[]{:S(2)}, u32[]{:S(2)}) %collective-permute-start.5) | collective-permute-done | bytes 1722400 | tf_op jit(solution)/shard_map/ppermute | solution.py:62
  135.7 5.0 collective-permute-start.13
  140.7 33.0 %collective-permute-done.6 = bf16[1,2,58,58,128]{4,1,3,2,0:T(2,128)(2,1)S(1)} collective-permute-done((bf16[1,2,58,58,128]{4,1,3,2,0:T(2,128)(2,1)S(1)}, bf16[1,2,58,58,128]{4,1,3,2,0:T(2,128)(2,1)S(1)}, u32[]{:S(2)}, u32[]{:S(2)}) %collective-permute-start.6) | collective-permute-done | bytes 1722400 | tf_op jit(solution)/shard_map/ppermute | solution.py:62
  175.1 5.2 collective-permute-start.14
  180.3 33.8 %collective-permute-done.7 = bf16[1,2,58,58,128]{4,1,3,2,0:T(2,128)(2,1)S(1)} collective-permute-done((bf16[1,2,58,58,128]{4,1,3,2,0:T(2,128)(2,1)S(1)}, bf16[1,2,58,58,128]{4,1,3,2,0:T(2,128)(2,1)S(1)}, u32[]{:S(2)}, u32[]{:S(2)}) %collective-permute-start.7) | collective-permute-done | bytes 1722400 | tf_op jit(solution)/shard_map/ppermute | solution.py:62
  215.8 5.2 collective-permute-start.15
  221.0 34.6 %collective-permute-done.8 = bf16[1,2,58,58,128]{4,1,3,2,0:T(2,128)(2,1)S(1)} collective-permute-done((bf16[1,2,58,58,128]{4,1,3,2,0:T(2,128)(2,1)S(1)}, bf16[1,2,58,58,128]{4,1,3,2,0:T(2,128)(2,1)S(1)}, u32[]{:S(2)}, u32[]{:S(2)}) %collective-permute-start.8) | collective-permute-done | bytes 1722400 | tf_op jit(solution)/shard_map/ppermute | solution.py:62
  257.5 5.3 collective-permute-start.16
  262.9 35.9 %collective-permute-done.9 = bf16[1,2,58,58,128]{4,1,3,2,0:T(2,128)(2,1)} collective-permute-done((bf16[1,2,58,58,128]{4,1,3,2,0:T(2,128)(2,1)S(1)}, bf16[1,2,58,58,128]{4,1,3,2,0:T(2,128)(2,1)}, u32[]{:S(2)}, u32[]{:S(2)}) %collective-permute-start.9) | collective-permute-done | bytes 1722400 | tf_op jit(solution)/shard_map/ppermute | solution.py:62
  308.8 4.8 collective-permute-start.17
  313.5 27.7 %collective-permute-done.10 = bf16[1,2,58,58,128]{4,1,3,2,0:T(2,128)(2,1)} collective-permute-done((bf16[1,2,58,58,128]{4,1,3,2,0:T(2,128)(2,1)}, bf16[1,2,58,58,128]{4,1,3,2,0:T(2,128)(2,1)}, u32[]{:S(2)}, u32[]{:S(2)}) %collective-permute-start.10) | collective-permute-done | bytes 1722400 | tf_op jit(solution)/shard_map/ppermute | solution.py:62
  353.8 5.4 fusion.56
  359.2 5.2 collective-permute-start.18
  364.4 18.3 %collective-permute-done.11 = bf16[1,2,58,58,128]{4,1,3,2,0:T(2,128)(2,1)} collective-permute-done((bf16[1,2,58,58,128]{4,1,3,2,0:T(2,128)(2,1)}, bf16[1,2,58,58,128]{4,1,3,2,0:T(2,128)(2,1)}, u32[]{:S(2)}, u32[]{:S(2)}) %collective-permute-start.11) | collective-permute-done | bytes 1722400 | tf_op jit(solution)/shard_map/ppermute | solution.py:62
  382.7 3.9 constant_dynamic-update-slice_fusion.31
  386.6 4.0 constant_dynamic-update-slice_fusion.30
  390.5 4.0 constant_dynamic-update-slice_fusion.29
  394.5 2.4 constant_dynamic-update-slice_fusion.28
  397.0 2.5 constant_dynamic-update-slice_fusion.27
  399.4 2.4 constant_dynamic-update-slice_fusion.26
  404.2 2.4 constant_dynamic-update-slice_fusion.24
  406.6 35.1 %constant_dynamic-update-slice_fusion.23 = bf16[32,2,58,58,128]{4,1,3,2,0:T(2,128)(2,1)} fusion(bf16[32,2,58,58,128]{4,1,3,2,0:T(2,128)(2,1)} %constant_dynamic-update-slice_fusion.24, bf16[2,15,58,128]{3,0,2,1:T(2,128)(2,1)S(1)} %collective-permute-done.3, bf16[2,28,15,128]{3,0,2,1:T(2,128)(2,1)S(1)} %collective-permute-done.1, ...), kind=kLoop, calls=%fused_computation.82 | loop fusion | flops 8611840 | bytes 3444736
  441.7 2.4 constant_dynamic-update-slice_fusion.22
  444.1 2.4 constant_dynamic-update-slice_fusion.21
  446.5 2.4 constant_dynamic-update-slice_fusion.20
  448.9 3.9 constant_dynamic-update-slice_fusion.19
  452.8 3.9 constant_dynamic-update-slice_fusion.18
  456.6 3.9 constant_dynamic-update-slice_fusion.17
  460.6 2.4 constant_dynamic-update-slice_fusion.16
  462.9 3.9 constant_dynamic-update-slice_fusion.15
  466.8 3.9 constant_dynamic-update-slice_fusion.14
  470.6 4.2 constant_dynamic-update-slice_fusion.13
  477.3 2.4 constant_dynamic-update-slice_fusion.11
  479.7 2.4 constant_dynamic-update-slice_fusion.10
  482.1 2.4 constant_dynamic-update-slice_fusion.9
  486.8 23.1 %constant_dynamic-update-slice_fusion.7 = bf16[32,2,58,58,128]{4,1,3,2,0:T(2,128)(2,1)} fusion(bf16[32,2,58,58,128]{4,1,3,2,0:T(2,128)(2,1)} %constant_dynamic-update-slice_fusion.8, bf16[2,15,58,128]{3,0,2,1:T(2,128)(2,1)S(1)} %collective-permute-done.3, bf16[2,28,15,128]{3,0,2,1:T(2,128)(2,1)S(1)} %collective-permute-done.1, ...), kind=kLoop, calls=%fused_computation.66 | loop fusion | flops 8611840 | bytes 3444736
  512.2 2.4 constant_dynamic-update-slice_fusion.5
  514.6 2.4 constant_dynamic-update-slice_fusion.4
  517.0 3.8 constant_dynamic-update-slice_fusion.3
  520.9 3.8 constant_dynamic-update-slice_fusion.2
  524.7 3.8 constant_dynamic-update-slice_fusion.1
  528.5 2.4 constant_dynamic-update-slice_fusion
  531.0 6.2 constant_dynamic-slice_fusion.4
  538.9 3.6 convolution_bitcast_fusion.2
  542.6 5.5 fusion.4
  548.0 3.8 fusion.29
  557.1 3.6 convolution_bitcast_fusion.1
  560.8 5.6 fusion.2
  566.4 3.3 fusion.28
  574.9 3.8 convolution_bitcast_fusion
  578.8 5.5 fusion
  584.2 3.3 fusion.27
  591.4 10.7 %multiply_add_fusion = f32[16,2,28,28,128]{4,1,3,2,0:T(2,128)} fusion(f32[2,28,28,128]{3,0,2,1:T(2,128)S(1)} %copy.34, f32[2,28,28,128]{3,0,2,1:T(2,128)S(1)} %copy.27, f32[2,28,28,128]{3,0,2,1:T(2,128)S(1)} %copy.20, f32[16]{0:T(128)S(1)} %copy-done.18, f32[16]{0:T(128)S(1)} %copy-done.19, f32[16]{0:T(128)S(1)} %copy-done.20), kind=kLoop, calls=%fused_computation | loop fusion | flops 16056320 | bytes 15253696 | tf_op jit(solution)/shard_map/add | solution.py:86
  604.8 179.7 %all-reduce.3.cloned.1.call-done = f32[16,2,28,28,128]{4,1,3,2,0:T(2,128)} async-done(((f32[16,2,28,28,128]{4,1,3,2,0:T(2,128)}), f32[16,2,28,28,128]{4,1,3,2,0:T(2,128)}) %all-reduce.3.cloned.1.call-update) | async-done | bytes 12845072
  784.5 3.1 fusion.40
  (99 shorter events, 52.7 us)
Async XLA Ops:
  6.5 778.0 %all-reduce.3.cloned.1.call-start = ((), (), s32[]{:S(2)}) async-start(), calls=%async_computation | async-start | bytes 25690112
  8.0 290.8 %copy-start.15 = (s32[1,1,3]{2,1,0:T(1,128)S(1)}, s32[1,1,3]{2,1,0:T(1,128)}, u32[]{:S(2)}) copy-start(s32[1,1,3]{2,1,0:T(1,128)} %param.12) | copy-start | bytes 40
  8.0 297.2 %copy-start.16 = (s32[1,1,3]{2,1,0:T(1,128)S(1)}, s32[1,1,3]{2,1,0:T(1,128)}, u32[]{:S(2)}) copy-start(s32[1,1,3]{2,1,0:T(1,128)} %param.11) | copy-start | bytes 40
  8.0 299.6 %copy-start.17 = (f32[6,3,31]{2,1,0:T(4,128)S(1)}, f32[6,3,31]{2,1,0:T(4,128)}, u32[]{:S(2)}) copy-start(f32[6,3,31]{2,1,0:T(4,128)} %param.9) | copy-start | bytes 6700
  8.3 8.0 %collective-permute-start = (bf16[2,28,15,128]{3,0,2,1:T(2,128)(2,1)S(1)}, bf16[2,28,15,128]{3,0,2,1:T(2,128)(2,1)S(1)}, u32[]{:S(2)}, u32[]{:S(2)}) collective-permute-start(bf16[2,28,15,128]{3,0,2,1:T(2,128)(2,1)S(1)} %get-tuple-element.22), channel_id=1, source_target_pairs={{0,8},{8,16},{16,24},{24,32},{32,40},{40,48},{48,56},{56,64},{64,7... | collective-permute-start | bytes 645128 | tf_op jit(solution)/shard_map/ppermute | solution.py:14
  12.3 7.7 collective-permute-start.1
  21.9 10.6 %collective-permute-start.2 = (bf16[2,15,58,128]{3,0,2,1:T(2,128)(2,1)S(1)}, bf16[2,15,58,128]{3,0,2,1:T(2,128)(2,1)S(1)}, u32[]{:S(2)}, u32[]{:S(2)}) collective-permute-start(bf16[2,15,58,128]{3,0,2,1:T(2,128)(2,1)S(1)} %get-tuple-element.20), channel_id=1, source_target_pairs={{0,1},{1,2},{2,3},{3,4},{4,5},{5,6},{6,7},{8,9},{9,10},{10,11},{11... | collective-permute-start | bytes 1336328 | tf_op jit(solution)/shard_map/ppermute | solution.py:14
  27.2 9.7 %collective-permute-start.3 = (bf16[2,15,58,128]{3,0,2,1:T(2,128)(2,1)S(1)}, bf16[2,15,58,128]{3,0,2,1:T(2,128)(2,1)S(1)}, u32[]{:S(2)}, u32[]{:S(2)}) collective-permute-start(bf16[2,15,58,128]{3,0,2,1:T(2,128)(2,1)S(1)} %get-tuple-element.21), channel_id=1, source_target_pairs={{1,0},{2,1},{3,2},{4,3},{5,4},{6,5},{7,6},{9,8},{10,9},{11,10},{12... | collective-permute-start | bytes 1336328 | tf_op jit(solution)/shard_map/ppermute | solution.py:15
  59.0 37.2 %collective-permute-start.4 = (bf16[1,2,58,58,128]{4,1,3,2,0:T(2,128)(2,1)S(1)}, bf16[1,2,58,58,128]{4,1,3,2,0:T(2,128)(2,1)S(1)}, u32[]{:S(2)}, u32[]{:S(2)}) collective-permute-start(bf16[1,2,58,58,128]{4,1,3,2,0:T(2,128)(2,1)S(1)} %maximum_bitcast_fusion), channel_id=1, source_target_pairs={{0,8},{8,16},{16,24},{24,32},{32,40},{40,48},{48,56},{56,64},{64,7... | collective-permute-start | bytes 5167112 | tf_op jit(solution)/shard_map/ppermute | solution.py:62
  96.2 38.2 %collective-permute-start.5 = (bf16[1,2,58,58,128]{4,1,3,2,0:T(2,128)(2,1)S(1)}, bf16[1,2,58,58,128]{4,1,3,2,0:T(2,128)(2,1)S(1)}, u32[]{:S(2)}, u32[]{:S(2)}) collective-permute-start(bf16[1,2,58,58,128]{4,1,3,2,0:T(2,128)(2,1)S(1)} %collective-permute-done.4), channel_id=1, source_target_pairs={{0,8},{8,16},{16,24},{24,32},{32,40},{40,48},{48,56},{56,64},{64,7... | collective-permute-start | bytes 5167112 | tf_op jit(solution)/shard_map/ppermute | solution.py:62
  96.2 38.2 %collective-permute-start.12 = (bf16[1,2,58,58,128]{4,1,3,2,0:T(2,128)(2,1)S(1)}, bf16[1,2,58,58,128]{4,1,3,2,0:T(2,128)(2,1)S(1)}, u32[]{:S(2)}, u32[]{:S(2)}) collective-permute-start(bf16[1,2,58,58,128]{4,1,3,2,0:T(2,128)(2,1)S(1)} %maximum_bitcast_fusion), channel_id=1, source_target_pairs={{0,120},{8,0},{16,8},{24,16},{32,24},{40,32},{48,40},{56,48},{64,5... | collective-permute-start | bytes 5167112 | tf_op jit(solution)/shard_map/ppermute | solution.py:64
  134.4 40.6 %copy-start.2 = (bf16[1,2,58,58,128]{4,1,3,2,0:T(2,128)(2,1)}, bf16[1,2,58,58,128]{4,1,3,2,0:T(2,128)(2,1)S(1)}, u32[]{:S(2)}) copy-start(bf16[1,2,58,58,128]{4,1,3,2,0:T(2,128)(2,1)S(1)} %collective-permute-done.5) | copy-start | bytes 5167108
  134.4 39.3 %collective-permute-start.6 = (bf16[1,2,58,58,128]{4,1,3,2,0:T(2,128)(2,1)S(1)}, bf16[1,2,58,58,128]{4,1,3,2,0:T(2,128)(2,1)S(1)}, u32[]{:S(2)}, u32[]{:S(2)}) collective-permute-start(bf16[1,2,58,58,128]{4,1,3,2,0:T(2,128)(2,1)S(1)} %collective-permute-done.5), channel_id=1, source_target_pairs={{0,8},{8,16},{16,24},{24,32},{32,40},{40,48},{48,56},{56,64},{64,7... | collective-permute-start | bytes 5167112 | tf_op jit(solution)/shard_map/ppermute | solution.py:62
  134.5 1.3 copy-start
  135.7 39.4 %collective-permute-start.13 = (bf16[1,2,58,58,128]{4,1,3,2,0:T(2,128)(2,1)S(1)}, bf16[1,2,58,58,128]{4,1,3,2,0:T(2,128)(2,1)S(1)}, u32[]{:S(2)}, u32[]{:S(2)}) collective-permute-start(bf16[1,2,58,58,128]{4,1,3,2,0:T(2,128)(2,1)S(1)} %collective-permute-done.12), channel_id=1, source_target_pairs={{0,120},{8,0},{16,8},{24,16},{32,24},{40,32},{48,40},{56,48},{64,5... | collective-permute-start | bytes 5167112 | tf_op jit(solution)/shard_map/ppermute | solution.py:64
  173.8 42.0 %copy-start.6 = (bf16[1,2,58,58,128]{4,1,3,2,0:T(2,128)(2,1)}, bf16[1,2,58,58,128]{4,1,3,2,0:T(2,128)(2,1)S(1)}, u32[]{:S(2)}) copy-start(bf16[1,2,58,58,128]{4,1,3,2,0:T(2,128)(2,1)S(1)} %collective-permute-done.6) | copy-start | bytes 5167108
  173.8 40.4 %collective-permute-start.7 = (bf16[1,2,58,58,128]{4,1,3,2,0:T(2,128)(2,1)S(1)}, bf16[1,2,58,58,128]{4,1,3,2,0:T(2,128)(2,1)S(1)}, u32[]{:S(2)}, u32[]{:S(2)}) collective-permute-start(bf16[1,2,58,58,128]{4,1,3,2,0:T(2,128)(2,1)S(1)} %collective-permute-done.6), channel_id=1, source_target_pairs={{0,8},{8,16},{16,24},{24,32},{32,40},{40,48},{48,56},{56,64},{64,7... | collective-permute-start | bytes 5167112 | tf_op jit(solution)/shard_map/ppermute | solution.py:62
  175.1 5.2 copy-start.4
  175.1 40.7 %collective-permute-start.14 = (bf16[1,2,58,58,128]{4,1,3,2,0:T(2,128)(2,1)S(1)}, bf16[1,2,58,58,128]{4,1,3,2,0:T(2,128)(2,1)S(1)}, u32[]{:S(2)}, u32[]{:S(2)}) collective-permute-start(bf16[1,2,58,58,128]{4,1,3,2,0:T(2,128)(2,1)S(1)} %collective-permute-done.13), channel_id=1, source_target_pairs={{0,120},{8,0},{16,8},{24,16},{32,24},{40,32},{48,40},{56,48},{64,5... | collective-permute-start | bytes 5167112 | tf_op jit(solution)/shard_map/ppermute | solution.py:64
  214.2 43.4 %copy-start.10 = (bf16[1,2,58,58,128]{4,1,3,2,0:T(2,128)(2,1)}, bf16[1,2,58,58,128]{4,1,3,2,0:T(2,128)(2,1)S(1)}, u32[]{:S(2)}) copy-start(bf16[1,2,58,58,128]{4,1,3,2,0:T(2,128)(2,1)S(1)} %collective-permute-done.7) | copy-start | bytes 5167108
  214.2 41.5 %collective-permute-start.8 = (bf16[1,2,58,58,128]{4,1,3,2,0:T(2,128)(2,1)S(1)}, bf16[1,2,58,58,128]{4,1,3,2,0:T(2,128)(2,1)S(1)}, u32[]{:S(2)}, u32[]{:S(2)}) collective-permute-start(bf16[1,2,58,58,128]{4,1,3,2,0:T(2,128)(2,1)S(1)} %collective-permute-done.7), channel_id=1, source_target_pairs={{0,8},{8,16},{16,24},{24,32},{32,40},{40,48},{48,56},{56,64},{64,7... | collective-permute-start | bytes 5167112 | tf_op jit(solution)/shard_map/ppermute | solution.py:62
  215.8 5.2 copy-start.8
  215.8 41.8 %collective-permute-start.15 = (bf16[1,2,58,58,128]{4,1,3,2,0:T(2,128)(2,1)S(1)}, bf16[1,2,58,58,128]{4,1,3,2,0:T(2,128)(2,1)}, u32[]{:S(2)}, u32[]{:S(2)}) collective-permute-start(bf16[1,2,58,58,128]{4,1,3,2,0:T(2,128)(2,1)S(1)} %collective-permute-done.14), channel_id=1, source_target_pairs={{0,120},{8,0},{16,8},{24,16},{32,24},{40,32},{48,40},{56,48},{64,5... | collective-permute-start | bytes 5167112 | tf_op jit(solution)/shard_map/ppermute | solution.py:64
  255.6 7.2 copy-start.12
  255.6 43.1 %collective-permute-start.9 = (bf16[1,2,58,58,128]{4,1,3,2,0:T(2,128)(2,1)S(1)}, bf16[1,2,58,58,128]{4,1,3,2,0:T(2,128)(2,1)}, u32[]{:S(2)}, u32[]{:S(2)}) collective-permute-start(bf16[1,2,58,58,128]{4,1,3,2,0:T(2,128)(2,1)S(1)} %collective-permute-done.8), channel_id=1, source_target_pairs={{0,8},{8,16},{16,24},{24,32},{32,40},{40,48},{48,56},{56,64},{64,7... | collective-permute-start | bytes 5167112 | tf_op jit(solution)/shard_map/ppermute | solution.py:62
  257.5 51.2 %collective-permute-start.16 = (bf16[1,2,58,58,128]{4,1,3,2,0:T(2,128)(2,1)}, bf16[1,2,58,58,128]{4,1,3,2,0:T(2,128)(2,1)}, u32[]{:S(2)}, u32[]{:S(2)}) collective-permute-start(bf16[1,2,58,58,128]{4,1,3,2,0:T(2,128)(2,1)} %collective-permute-done.15), channel_id=1, source_target_pairs={{0,120},{8,0},{16,8},{24,16},{32,24},{40,32},{48,40},{56,48},{64,5... | collective-permute-start | bytes 5167112 | tf_op jit(solution)/shard_map/ppermute | solution.py:64
  298.8 42.4 %collective-permute-start.10 = (bf16[1,2,58,58,128]{4,1,3,2,0:T(2,128)(2,1)}, bf16[1,2,58,58,128]{4,1,3,2,0:T(2,128)(2,1)}, u32[]{:S(2)}, u32[]{:S(2)}) collective-permute-start(bf16[1,2,58,58,128]{4,1,3,2,0:T(2,128)(2,1)} %collective-permute-done.9), channel_id=1, source_target_pairs={{0,8},{8,16},{16,24},{24,32},{32,40},{40,48},{48,56},{56,64},{64,7... | collective-permute-start | bytes 5167112 | tf_op jit(solution)/shard_map/ppermute | solution.py:62
  308.8 50.5 %collective-permute-start.17 = (bf16[1,2,58,58,128]{4,1,3,2,0:T(2,128)(2,1)}, bf16[1,2,58,58,128]{4,1,3,2,0:T(2,128)(2,1)}, u32[]{:S(2)}, u32[]{:S(2)}) collective-permute-start(bf16[1,2,58,58,128]{4,1,3,2,0:T(2,128)(2,1)} %collective-permute-done.16), channel_id=1, source_target_pairs={{0,120},{8,0},{16,8},{24,16},{32,24},{40,32},{48,40},{56,48},{64,5... | collective-permute-start | bytes 5167112 | tf_op jit(solution)/shard_map/ppermute | solution.py:64
  341.2 41.5 %collective-permute-start.11 = (bf16[1,2,58,58,128]{4,1,3,2,0:T(2,128)(2,1)}, bf16[1,2,58,58,128]{4,1,3,2,0:T(2,128)(2,1)}, u32[]{:S(2)}, u32[]{:S(2)}) collective-permute-start(bf16[1,2,58,58,128]{4,1,3,2,0:T(2,128)(2,1)} %collective-permute-done.10), channel_id=1, source_target_pairs={{0,8},{8,16},{16,24},{24,32},{32,40},{40,48},{48,56},{56,64},{64,7... | collective-permute-start | bytes 5167112 | tf_op jit(solution)/shard_map/ppermute | solution.py:62
  359.2 101.3 %collective-permute-start.18 = (bf16[1,2,58,58,128]{4,1,3,2,0:T(2,128)(2,1)}, bf16[1,2,58,58,128]{4,1,3,2,0:T(2,128)(2,1)S(1)}, u32[]{:S(2)}, u32[]{:S(2)}) collective-permute-start(bf16[1,2,58,58,128]{4,1,3,2,0:T(2,128)(2,1)} %collective-permute-done.17), channel_id=1, source_target_pairs={{0,120},{8,0},{16,8},{24,16},{32,24},{40,32},{48,40},{56,48},{64,5... | collective-permute-start | bytes 5167112 | tf_op jit(solution)/shard_map/ppermute | solution.py:64
  386.6 8.0 %copy-start.13 = (bf16[1,2,58,58,128]{4,1,3,2,0:T(2,128)(2,1)S(1)}, bf16[1,2,58,58,128]{4,1,3,2,0:T(2,128)(2,1)}, u32[]{:S(2)}) copy-start(bf16[1,2,58,58,128]{4,1,3,2,0:T(2,128)(2,1)} %copy-done.12) | copy-start | bytes 5167108
  390.5 6.4 copy-start.11
  394.5 4.9 copy-start.7
  396.9 4.9 copy-start.3
  404.2 37.6 %copy-start.1 = (bf16[1,2,58,58,128]{4,1,3,2,0:T(2,128)(2,1)S(1)}, bf16[1,2,58,58,128]{4,1,3,2,0:T(2,128)(2,1)}, u32[]{:S(2)}) copy-start(bf16[1,2,58,58,128]{4,1,3,2,0:T(2,128)(2,1)} %copy-done) | copy-start | bytes 5167108
  406.6 37.5 %copy-start.5 = (bf16[1,2,58,58,128]{4,1,3,2,0:T(2,128)(2,1)S(1)}, bf16[1,2,58,58,128]{4,1,3,2,0:T(2,128)(2,1)}, u32[]{:S(2)}) copy-start(bf16[1,2,58,58,128]{4,1,3,2,0:T(2,128)(2,1)} %copy-done.4) | copy-start | bytes 5167108
  441.7 4.8 copy-start.9
  587.6 3.8 copy-start.18
  587.6 3.8 copy-start.19
  587.6 3.8 copy-start.20
  602.1 0.7 copy-start.21
  602.1 1.9 copy-start.22
  602.1 182.4 %copy-start.14 = (f32[2,28,28,128]{3,0,2,1:T(2,128)S(1)}, f32[2,28,28,128]{3,0,2,1:T(2,128)}, u32[]{:S(2)}) copy-start(f32[2,28,28,128]{3,0,2,1:T(2,128)} %param.7) | copy-start | bytes 2408452
Sparse Core Ops, SparseCore 0:
  602.3 182.1 all-reduce.2
